TPU v7x, 512 devices: a whole 4x4x16 slice. The times are simulated.
512 devices in a mesh: vol: 8 (over x, core), row: 16 (over y, z_hi), col: 4 (over z_lo).
Axes of the slice: x: 4, y: 4, z: 16 (z_hi: 4, z_lo: 4; z = z_hi * 4 + z_lo), core: 2. Of those that a mesh axis runs over, the one named last changes fastest.
Arguments:
- source: float32 [16, 64, 128, 512], P(None, 'vol', 'row', 'col'), may hold values from -8 to 8
- labels: int32 [64, 128, 512], P('vol', 'row', 'col'), may hold values from 0 to 7
- region_coeff: float32 [8], replicated, may hold values from 0.3 to 3
- node_cell: int32 [65536], P(('vol', 'row', 'col')), may hold values from 0 to 8191
- node_pos: float32 [3, 65536], P(None, ('vol', 'row', 'col')), may hold values from 0 to 1
- incident: float32 [16, 65536], P(None, ('vol', 'row', 'col')), may hold values from -6 to 6
Outputs:
- field: float32 [16, 64, 128, 512], P(None, 'vol', 'row', 'col')
- flux: float32 [16, 65536], P(None, ('vol', 'row', 'col'))
Inputs may be any that keep to these rules, and one draw needn't show every extreme that they name: `node_cell`: cell of node j inside its volume block, several nodes may share a cell.
All inputs are finite; a program needn't handle non-finite values.
Results may differ from a plain program's by a relative error of at most 0.0029.
Values may be sent and summed in bfloat16 or wider, within the bound.
A program may use at most 64 MiB of HBM per device.

v0:
```python
import functools
import math

import jax
import jax.numpy as jnp
from jax import lax
from jax.sharding import PartitionSpec as P

SWEEPS = 4
ITERS = 2


MASS_TERM = 0.05
SOFTENING = 0.05
KERNEL_GAIN = 2.0
COUPLING = 1.0


def padded_2(cells, sides, width):
    for axis, dim in sides:
        count = lax.axis_size(axis)
        ends = count - 1
        head = lax.slice_in_dim(cells, 0, width, axis=dim)
        tail = lax.slice_in_dim(cells, cells.shape[dim] - width, cells.shape[dim], axis=dim)
        cells = jnp.concatenate(
            [
                lax.ppermute(tail, axis, [(i, (i + 1) % count) for i in range(ends)]),
                cells,
                lax.ppermute(head, axis, [((i + 1) % count, i) for i in range(ends)]),
            ],
            axis=dim,
        )
    return cells


def sweep_weights(count):
    return [
        1.0 / (1.05 - 0.95 * math.cos(math.pi * (2 * sweep + 1) / (2 * count)))
        for sweep in range(count)
    ]


def face_terms(kcoef):
    padded = padded_2(kcoef, (("vol", 0), ("row", 1), ("col", 2)), 1)
    neighbours = [
        padded[2:, 1:-1, 1:-1],
        padded[:-2, 1:-1, 1:-1],
        padded[1:-1, 2:, 1:-1],
        padded[1:-1, :-2, 1:-1],
        padded[1:-1, 1:-1, 2:],
        padded[1:-1, 1:-1, :-2],
    ]
    faces = [0.5 * (kcoef + other) for other in neighbours]
    diag = MASS_TERM + faces[0]
    for other in faces[1:]:
        diag = diag + other
    return (faces, diag)


def operate(values, faces, diag):
    padded = padded_2(values, (("vol", 1), ("row", 2), ("col", 3)), 1)
    neighbours = [
        padded[:, 2:, 1:-1, 1:-1],
        padded[:, :-2, 1:-1, 1:-1],
        padded[:, 1:-1, 2:, 1:-1],
        padded[:, 1:-1, :-2, 1:-1],
        padded[:, 1:-1, 1:-1, 2:],
        padded[:, 1:-1, 1:-1, :-2],
    ]
    total = faces[0] * neighbours[0]
    for number in range(1, 6):
        total = total + faces[number] * neighbours[number]
    return diag * values - total


def accumulate(carry, piece, start, column_pos, row_pos, scale):
    count = piece.shape[1]
    blocking = math.gcd(count, 2048)
    wide_piece = lax.optimization_barrier(piece).astype(jnp.float32)

    def one_block(position, total):
        offset = position * blocking
        trace_block = lax.dynamic_slice_in_dim(wide_piece, offset, blocking, 1)
        point_block = lax.dynamic_slice_in_dim(column_pos, offset, blocking, 1)
        delta_x = point_block[0][:, None] - row_pos[0][None, :]
        delta_y = point_block[1][:, None] - row_pos[1][None, :]
        delta_z = point_block[2][:, None] - row_pos[2][None, :]
        squared = delta_x * delta_x + delta_y * delta_y + delta_z * delta_z
        tile = (scale * lax.rsqrt(squared + SOFTENING * SOFTENING)).astype(jnp.bfloat16)
        wide_tile = lax.optimization_barrier(tile).astype(jnp.float32)
        return total + jnp.dot(trace_block, wide_tile, preferred_element_type=jnp.float32)

    return lax.fori_loop(0, count // blocking, one_block, carry)


def per_device(source, labels, region_coeff, node_cell, node_pos, incident):
    kcoef = jnp.zeros(labels.shape, jnp.float32)
    for region in range(region_coeff.shape[0]):
        kcoef = jnp.where(labels == region, region_coeff[region], kcoef)
    faces, diag = face_terms(kcoef)
    node_count = node_cell.shape[0]
    all_nodes = node_count * lax.axis_size("vol") * lax.axis_size("row") * lax.axis_size("col")
    scale = KERNEL_GAIN / math.sqrt(all_nodes)
    row_pos = lax.all_gather(node_pos, "col", axis=1, tiled=True)
    column_pos = lax.all_gather(node_pos, ("vol", "row"), axis=1, tiled=True)
    folding = functools.partial(accumulate, column_pos=column_pos, row_pos=row_pos, scale=scale)
    channels = source.shape[0]
    field = jnp.zeros(source.shape, jnp.float32)
    flux = incident
    weights = sweep_weights(SWEEPS)
    for outer in range(ITERS):
        rhs = (
            source.reshape(channels, -1).at[:, node_cell].add(COUPLING * flux).reshape(source.shape)
        )
        for weight in weights:
            field = field + weight * (rhs - operate(field, faces, diag)) / diag
        traces = field.reshape(channels, -1)[:, node_cell].astype(jnp.bfloat16)
        initial = jnp.zeros((channels, row_pos.shape[1]), jnp.float32)
        partial_flux = folding(
            initial, lax.all_gather(traces, ("vol", "row"), axis=1, tiled=True), jnp.int32(0)
        )
        own_flux = lax.psum_scatter(partial_flux, "col", scatter_dimension=1, tiled=True)
        flux = incident + own_flux
    return (field, flux)


def solution(mesh):
    placed = (
        P(None, "vol", "row", "col"),
        P("vol", "row", "col"),
        P(),
        P(("vol", "row", "col")),
        P(None, ("vol", "row", "col")),
        P(None, ("vol", "row", "col")),
    )
    return jax.shard_map(
        per_device,
        mesh=mesh,
        in_specs=placed,
        out_specs=(P(None, "vol", "row", "col"), P(None, ("vol", "row", "col"))),
        check_vma=False,
    )
```

profile of v0, /device:TPU:1, one launch (start us, length us, event | category | flops | bytes accessed | tf_op | source)
XLA Modules:
  0.0 1818.4 jit_solution(9501266454963995164)
XLA Ops:
  8.8 5.8 select_select_fusion
  14.7 8.7 collective-permute-start
  32.3 7.9 collective-permute-start.3
  44.5 4.5 copy.78
  49.1 5.4 scatter_fusion
  64.1 7.9 collective-permute-start.9
  72.7 4.4 collective-permute-done.8
  99.0 8.7 collective-permute-start.15
  107.7 5.2 collective-permute-done.14
  135.8 8.3 collective-permute-start.21
  144.1 4.3 collective-permute-done.20
  165.5 5.1 collective-permute-start.25
  173.2 8.7 collective-permute-start.27
  191.0 413.1 %all_gather.13 = f32[3,16384]{1,0:T(4,128)} all-gather(f32[3,128]{1,0:T(4,128)S(1)} %copy-done.51), channel_id=1, replica_groups=mesh['vol'=8,'row'=16,'col'=4] {'vol','row'}, dimensions={1}, use_global_device_ids=true | all-gather | bytes 198144 | tf_op jit(solution)/shard_map/all_gather | solution.py:105
  604.1 10.2 all_gather.14
  619.6 27.0 %collective-permute-start.30 = (f32[16,1,8,128]{3,0,2,1:T(8,128)}, f32[16,1,8,128]{3,0,2,1:T(8,128)S(1)}, u32[]{:S(2)}, u32[]{:S(2)}) collective-permute-start(f32[16,1,8,128]{3,0,2,1:T(8,128)} %get-tuple-element.329), channel_id=1, source_target_pairs={{64,0},{128,64},{192,128},{256,192},{320,256},{384,320},{448,384},... | collective-permute-start | bytes 196616 | tf_op jit(solution)/shard_map/ppermute | solution.py:29
  649.4 442.3 %all_gather.12 = bf16[16,16384]{0,1:T(8,128)(2,1)} all-gather(bf16[16,128]{0,1:T(8,128)(2,1)S(1)} %bitcast.84), channel_id=1, replica_groups=mesh['vol'=8,'row'=16,'col'=4] {'vol','row'}, dimensions={1}, use_global_device_ids=true | all-gather | bytes 528384 | tf_op jit(solution)/shard_map/all_gather | solution.py:120
  1097.2 8.9 collective-permute-start.33
  1106.1 26.3 %while.28 = (s32[]{:T(128)}, f32[16,512]{1,0:T(8,128)S(1)}, bf16[16,16384]{1,0:T(8,128)(2,1)S(1)}, f32[3,16384]{1,0:T(4,128)}, f32[3,512]{1,0:T(4,128)S(1)}, /*i...) while((s32[]{:T(128)}, f32[16,512]{1,0:T(8,128)S(1)}, ...), condition=%wide.region_2.3_spmd.clone, body=%wide.region_1.2_spmd.clone.sunk | while | flops 45105160 | bytes 4417749 | solution.py:93
  1140.1 27.5 %reduce-scatter.3.cloned.1.call-done = f32[16,128]{1,0:T(8,128)} async-done(((f32[16,512]{1,0:T(8,128)}), f32[16,128]{1,0:T(8,128)}) %reduce-scatter.3.cloned.1.call-update) | async-done | bytes 8208 | tf_op jit(solution)/shard_map/reduce_scatter | solution.py:122
  1168.3 5.5 scatter_fusion.1
  1180.3 4.9 collective-permute-start.36
  1190.8 8.2 collective-permute-start.39
  1199.0 4.2 collective-permute-done.38
  1225.8 8.0 collective-permute-start.45
  1236.7 8.2 collective-permute-start.47
  1263.6 8.8 collective-permute-start.51
  1276.7 5.0 collective-permute-start.53
  1284.3 4.0 collective-permute-done.53
  1293.9 444.7 %all_gather.15 = bf16[16,16384]{0,1:T(8,128)(2,1)} all-gather(bf16[16,128]{0,1:T(8,128)(2,1)S(1)} %bitcast.83), channel_id=1, replica_groups=mesh['vol'=8,'row'=16,'col'=4] {'vol','row'}, dimensions={1}, use_global_device_ids=true | all-gather | bytes 528384 | tf_op jit(solution)/shard_map/all_gather | solution.py:120
  1742.0 26.4 %while.29 = (s32[]{:T(128)}, f32[16,512]{1,0:T(8,128)S(1)}, bf16[16,16384]{1,0:T(8,128)(2,1)S(1)}, f32[3,16384]{1,0:T(4,128)}, f32[3,512]{1,0:T(4,128)S(1)}, /*i...) while((s32[]{:T(128)}, f32[16,512]{1,0:T(8,128)S(1)}, ...), condition=%wide.region_6.7_spmd.clone, body=%wide.region_5.6_spmd.clone.sunk | while | flops 45105160 | bytes 4417749 | solution.py:93
  1770.0 40.0 %reduce-scatter.5.cloned.1.call-done = f32[16,128]{1,0:T(8,128)} async-done(((f32[16,512]{1,0:T(8,128)}), f32[16,128]{1,0:T(8,128)}) %reduce-scatter.5.cloned.1.call-update) | async-done | bytes 8208 | tf_op jit(solution)/shard_map/reduce_scatter | solution.py:122
  (362 shorter events, 246.6 us)
Async XLA Ops:
  7.2 1160.4 %reduce-scatter.3.cloned.1.call-start = ((), (), s32[]{:S(2)}) async-start(), calls=%async_computation.2 | async-start | bytes 40960 | tf_op jit(solution)/shard_map/reduce_scatter | solution.py:122
  14.7 16.3 collective-permute-start
  25.4 37.3 %collective-permute-start.6 = (f32[16,1,8,128]{3,0,2,1:T(8,128)S(1)}, f32[16,1,8,128]{3,0,2,1:T(8,128)S(1)}, u32[]{:S(2)}, u32[]{:S(2)}) collective-permute-start(f32[16,1,8,128]{3,0,2,1:T(8,128)S(1)} %broadcast.70), channel_id=1, source_target_pairs={{64,0},{128,64},{192,128},{256,192},{320,256},{384,320},{448,384},... | collective-permute-start | bytes 196616 | tf_op jit(solution)/shard_map/ppermute | solution.py:29
  27.8 34.9 %collective-permute-start.7 = (f32[16,1,8,128]{3,0,2,1:T(8,128)S(1)}, f32[16,1,8,128]{3,0,2,1:T(8,128)S(1)}, u32[]{:S(2)}, u32[]{:S(2)}) collective-permute-start(f32[16,1,8,128]{3,0,2,1:T(8,128)S(1)} %broadcast.70), channel_id=1, source_target_pairs={{0,64},{64,128},{128,192},{192,256},{256,320},{320,384},{384,448},... | collective-permute-start | bytes 196616 | tf_op jit(solution)/shard_map/ppermute | solution.py:27
  31.0 26.2 %collective-permute-start.2 = (f32[10,1,128]{2,1,0:T(1,128)S(1)}, f32[10,1,128]{2,1,0:T(1,128)S(1)}, u32[]{:S(2)}, u32[]{:S(2)}) collective-permute-start(f32[10,1,128]{2,1,0:T(1,128)S(1)} %get-tuple-element.339), channel_id=1, source_target_pairs={{4,0},{8,4},{12,8},{16,12},{20,16},{24,20},{28,24},{32,28},{36,32}... | collective-permute-start | bytes 15368 | tf_op jit(solution)/shard_map/ppermute | solution.py:29
  32.3 24.9 %collective-permute-start.3 = (f32[10,1,128]{2,1,0:T(1,128)S(1)}, f32[10,1,128]{2,1,0:T(1,128)S(1)}, u32[]{:S(2)}, u32[]{:S(2)}) collective-permute-start(f32[10,1,128]{2,1,0:T(1,128)S(1)} %get-tuple-element.338), channel_id=1, source_target_pairs={{0,4},{4,8},{8,12},{12,16},{16,20},{20,24},{24,28},{28,32},{32,36}... | collective-permute-start | bytes 15368 | tf_op jit(solution)/shard_map/ppermute | solution.py:27
  57.4 14.6 collective-permute-start.4
  58.7 13.3 collective-permute-start.5
  62.8 14.4 collective-permute-start.8
  64.1 13.1 collective-permute-start.9
  97.7 15.2 collective-permute-start.14
  99.0 13.9 collective-permute-start.15
  134.5 13.9 collective-permute-start.20
  135.8 12.6 collective-permute-start.21
  171.9 10.6 collective-permute-start.26
  173.2 10.2 collective-permute-start.27
  184.8 429.5 %collective-permute-start.29 = (f32[16,10,10,1]{2,0,3,1:T(8,128)S(1)}, f32[16,10,10,1]{2,0,3,1:T(8,128)S(1)}, u32[]{:S(2)}, u32[]{:S(2)}) collective-permute-start(f32[16,10,10,1]{2,0,3,1:T(8,128)S(1)} %copy.42), channel_id=1, source_target_pairs={{0,1},{1,2},{2,3},{4,5},{5,6},{6,7},{8,9},{9,10},{10,11},{12,13},{... | collective-permute-start | bytes 19208 | tf_op jit(solution)/shard_map/ppermute | solution.py:27
  189.7 425.6 %collective-permute-start.28 = (f32[16,10,10,1]{2,0,3,1:T(8,128)S(1)}, f32[16,10,10,1]{2,0,3,1:T(8,128)S(1)}, u32[]{:S(2)}, u32[]{:S(2)}) collective-permute-start(f32[16,10,10,1]{2,0,3,1:T(8,128)S(1)} %copy.40), channel_id=1, source_target_pairs={{1,0},{2,1},{3,2},{5,4},{6,5},{7,6},{9,8},{10,9},{11,10},{13,12},{... | collective-permute-start | bytes 19208 | tf_op jit(solution)/shard_map/ppermute | solution.py:29
  619.6 475.6 %collective-permute-start.30 = (f32[16,1,8,128]{3,0,2,1:T(8,128)}, f32[16,1,8,128]{3,0,2,1:T(8,128)S(1)}, u32[]{:S(2)}, u32[]{:S(2)}) collective-permute-start(f32[16,1,8,128]{3,0,2,1:T(8,128)} %get-tuple-element.329), channel_id=1, source_target_pairs={{64,0},{128,64},{192,128},{256,192},{320,256},{384,320},{448,384},... | collective-permute-start | bytes 196616 | tf_op jit(solution)/shard_map/ppermute | solution.py:29
  646.6 448.6 %collective-permute-start.31 = (f32[16,1,8,128]{3,0,2,1:T(8,128)S(1)}, f32[16,1,8,128]{3,0,2,1:T(8,128)S(1)}, u32[]{:S(2)}, u32[]{:S(2)}) collective-permute-start(f32[16,1,8,128]{3,0,2,1:T(8,128)S(1)} %get-tuple-element.328), channel_id=1, source_target_pairs={{0,64},{64,128},{128,192},{192,256},{256,320},{320,384},{384,448},... | collective-permute-start | bytes 196616 | tf_op jit(solution)/shard_map/ppermute | solution.py:27
  1095.9 37.2 %collective-permute-start.32 = (f32[16,10,1,128]{3,0,2,1:T(8,128)}, f32[16,10,1,128]{3,0,2,1:T(8,128)S(1)}, u32[]{:S(2)}, u32[]{:S(2)}) collective-permute-start(f32[16,10,1,128]{3,0,2,1:T(8,128)} %get-tuple-element.313), channel_id=1, source_target_pairs={{4,0},{8,4},{12,8},{16,12},{20,16},{24,20},{28,24},{32,28},{36,32}... | collective-permute-start | bytes 245768 | tf_op jit(solution)/shard_map/ppermute | solution.py:29
  1097.2 36.0 %collective-permute-start.33 = (f32[16,10,1,128]{3,0,2,1:T(8,128)}, f32[16,10,1,128]{3,0,2,1:T(8,128)}, u32[]{:S(2)}, u32[]{:S(2)}) collective-permute-start(f32[16,10,1,128]{3,0,2,1:T(8,128)} %get-tuple-element.312), channel_id=1, source_target_pairs={{0,4},{4,8},{8,12},{12,16},{16,20},{20,24},{24,28},{28,32},{32,36}... | collective-permute-start | bytes 245768 | tf_op jit(solution)/shard_map/ppermute | solution.py:27
  1133.1 676.9 %reduce-scatter.5.cloned.1.call-start = ((), (), s32[]{:S(2)}) async-start(), calls=%async_computation.3 | async-start | bytes 40960 | tf_op jit(solution)/shard_map/reduce_scatter | solution.py:122
  1135.6 41.1 %collective-permute-start.35 = (f32[16,10,10,1]{2,0,3,1:T(8,128)S(1)}, f32[16,10,10,1]{2,0,3,1:T(8,128)S(1)}, u32[]{:S(2)}, u32[]{:S(2)}) collective-permute-start(f32[16,10,10,1]{2,0,3,1:T(8,128)S(1)} %copy.50), channel_id=1, source_target_pairs={{0,1},{1,2},{2,3},{4,5},{5,6},{6,7},{8,9},{9,10},{10,11},{12,13},{... | collective-permute-start | bytes 19208 | tf_op jit(solution)/shard_map/ppermute | solution.py:27
  1138.8 39.0 %collective-permute-start.34 = (f32[16,10,10,1]{2,0,3,1:T(8,128)S(1)}, f32[16,10,10,1]{2,0,3,1:T(8,128)S(1)}, u32[]{:S(2)}, u32[]{:S(2)}) collective-permute-start(f32[16,10,10,1]{2,0,3,1:T(8,128)S(1)} %copy.48), channel_id=1, source_target_pairs={{1,0},{2,1},{3,2},{5,4},{6,5},{7,6},{9,8},{10,9},{11,10},{13,12},{... | collective-permute-start | bytes 19208 | tf_op jit(solution)/shard_map/ppermute | solution.py:29
  1189.5 13.7 collective-permute-start.38
  1190.8 12.4 collective-permute-start.39
  1225.8 9.5 collective-permute-start.45
  1236.7 13.9 collective-permute-start.47
  1262.3 13.0 collective-permute-start.50
  1263.6 11.7 collective-permute-start.51
  1276.7 11.7 collective-permute-start.53
  (78 other events, 5458.5 us)
Sparse Core Ops, SparseCore 0:
  1133.3 34.2 reduce-scatter.2
  1769.2 40.8 reduce-scatter.4
where the time goes:
time: 1830 us; the launch traced here: 1820 us
  blocking collectives  1310 us (72%)
  starting transfers between devices  214 us (12%)
  waiting for transfers between devices  121 us (7%)
  local copies, waits for them, and re-layouts  86.2 us (5%)
  other arithmetic  64.6 us (4%)
    all_gather x2, blocking collectives, per_device(): lax.all_gather(traces, ('vol', 'row'), axis=1, tiled=True)  887 us
    all_gather x1, blocking collectives, per_device(): column_pos = lax.all_gather(node_pos, ('vol', 'row'), axis=1, tiled=True)  413 us
    ppermute x27, starting transfers between devices, padded_2(): lax.ppermute(tail, axis, [(i, (i + 1) % count) for i in range(ends)])  133 us
    ppermute x27, starting transfers between devices, padded_2(): lax.ppermute(head, axis, [((i + 1) % count, i) for i in range(ends)])  81 us
    reduce_scatter x2, waiting for transfers between devices, per_device(): lax.psum_scatter(partial_flux, 'col', scatter_dimension=1, tiled=True)  67.5 us
  transfers between devices with their start and end apart: 56, of which 25 were waited for; matrix products, arithmetic and copies ran while one was open for 4% of the time, Pallas kernels for 0%

commit v1 on v0

v1 whole, which is shorter than its diff:
```python
import functools
import math

import jax
import jax.numpy as jnp
from jax import lax
from jax.experimental import pallas as pl
from jax.experimental.pallas import tpu as pltpu
from jax.sharding import PartitionSpec as P

SWEEPS = 4
ITERS = 2

MASS_TERM = 0.05
SOFTENING = 0.05
KERNEL_GAIN = 2.0

MESH = pl.DeviceIdType.MESH
F32 = jnp.float32
BF16 = jnp.bfloat16

E, CX, CY, CZ, ND = 16, 8, 8, 128, 128
STEPS = SWEEPS * ITERS
HALOS = STEPS - 1


def sweep_weights(count):
    return [
        1.0 / (1.05 - 0.95 * math.cos(math.pi * (2 * sweep + 1) / (2 * count)))
        for sweep in range(count)
    ]


class Plan:
    def __init__(self, mesh):
        self.n_vol, self.n_row, self.n_col = (mesh.shape[a] for a in ("vol", "row", "col"))
        self.z_hi = 4 if self.n_row == 16 else 2
        self.n_y = self.n_row // self.z_hi
        self.n_z = self.z_hi * self.n_col
        half = self.n_z // 2
        order = []
        for d in range(1, half):
            order += [d, self.n_z - d]
        order += [0, half]
        self.z_deltas = order
        self.z_own = order.index(0)
        self.n_q = self.n_z // 2
        ring = lambda d, n: min(d, n - d)
        plane = [(dv, dy) for dv in range(self.n_vol) for dy in range(self.n_y)]
        plane.sort(key=lambda p: -(ring(p[0], self.n_vol) / 2 + ring(p[1], self.n_y)))
        self.p_deltas = plane
        self.p_own = plane.index((0, 0))
        self.n_p = len(plane)
        self.n_m = self.n_p // 2
        self.nodes = ND * self.n_vol * self.n_row * self.n_col

    def here(self):
        v, r, c = (lax.axis_index(a) for a in ("vol", "row", "col"))
        self.v, self.r, self.c = v, r, c
        self.y = lax.div(r, self.z_hi)
        self.zh = lax.rem(r, self.z_hi)
        self.z = self.zh * self.n_col + c

    def z_peer(self, delta):
        zz = lax.rem(self.z + delta, self.n_z)
        return (self.v, self.y * self.z_hi + lax.div(zz, self.n_col), lax.rem(zz, self.n_col))

    def p_peer(self, delta):
        dv, dy = delta
        return (
            lax.rem(self.v + dv, self.n_vol),
            lax.rem(self.y + dy, self.n_y) * self.z_hi + self.zh,
            self.c,
        )

    def z_slot_of_me_at(self, delta):
        return self.z_deltas.index((self.n_z - delta) % self.n_z)

    def p_slot_of_me_at(self, delta):
        return self.p_deltas.index(((self.n_vol - delta[0]) % self.n_vol, (self.n_y - delta[1]) % self.n_y))

    def sides(self):
        up = lambda i, n: lax.rem(i + 1, n)
        down = lambda i, n: lax.rem(i + n - 1, n)
        v, r, c = self.v, self.r, self.c
        return (
            (up(v, self.n_vol), r, c),
            (down(v, self.n_vol), r, c),
            (v, up(r, self.n_row), c),
            (v, down(r, self.n_row), c),
            (v, r, up(c, self.n_col)),
            (v, r, down(c, self.n_col)),
        )


def kernel(
    plan, source, labels, coeff, cell, pos, incident, field_out, flux_out,
    F, S, B, KC, KYS, KYR, KZS, KZR, CO, DI, YS, YR, ZS, ZR, OH, TR, ACC, RR, G, POSZ, POSP, PJ,
    src_sem, out_sem, k_ss, k_rs, h_ss, h_rs, pz_ss, pz_rs, pp_ss, pp_rs, t_ss, t_rs, r_ss, r_rs,
):
    plan.here()
    weights = sweep_weights(SWEEPS) * ITERS
    lanes = lax.broadcasted_iota(jnp.int32, (8, 128), 1)
    subs = lax.broadcasted_iota(jnp.int32, (8, 128), 0)
    sides = plan.sides()
    n_q, n_m, n_p, n_z = plan.n_q, plan.n_m, plan.n_p, plan.n_z

    def source_copy(x, y):
        return pltpu.make_async_copy(source.at[:, x, y, :], S.at[x, y], src_sem)

    def field_copy(x, y):
        return pltpu.make_async_copy(F.at[STEPS - 1, x + 1, y + 1], field_out.at[:, x, y, :], out_sem)

    def over_blocks(act):
        def body(x, _):
            for y in range(CY):
                act(x, y)
            return 0

        lax.fori_loop(0, CX, body, 0)

    over_blocks(lambda x, y: source_copy(x, y).start())

    barrier = pltpu.get_barrier_semaphore()
    peers = [plan.z_peer(d) for d in plan.z_deltas if d]
    peers += [plan.p_peer(d) for d in plan.p_deltas if d != (0, 0)]
    peers += [sides[2], sides[3]]
    for peer in peers:
        pl.semaphore_signal(barrier, inc=1, device_id=peer, device_id_type=MESH)

    kz_up = jnp.zeros((8, 128), F32)
    kz_down = jnp.zeros((8, 128), F32)
    for x in range(CX):
        label = labels[x]
        k = jnp.zeros((8, 128), F32)
        for region in range(8):
            k = jnp.where(label == region, coeff[region], k)
        KC[x + 1] = k
        KYS[0, x] = k[CY - 1]
        KYS[1, x] = k[0]
        kz_up = jnp.where(lanes == x, pltpu.roll(k, x + 1, 1), kz_up)
        kz_down = jnp.where(lanes == x, pltpu.roll(k, x, 1), kz_down)
    KZS[0] = kz_up
    KZS[1] = kz_down

    inverse_scale = math.sqrt(plan.nodes) / KERNEL_GAIN
    own_pos = jnp.concatenate([pos[...] * inverse_scale, jnp.zeros((5, 128), F32)], axis=0)
    POSZ[plan.z_own] = own_pos
    POSP[plan.p_own] = own_pos
    cells = jnp.broadcast_to(cell[...], (8, 128))
    rows = lax.div(cells, CZ)
    rows16 = jnp.concatenate([rows, rows], axis=0)
    z_of = lax.rem(cells, CZ)
    for block in range(CZ // 16):
        z_pair = jnp.concatenate([z_of - subs - 16 * block, z_of - subs - 16 * block - 8], axis=0)
        OH[16 * block : 16 * block + 16, :] = jnp.where(z_pair == 0, 1.0, 0.0).astype(BF16)

    pl.semaphore_wait(barrier, len(peers))

    def k_copy(side):
        src, dst = (
            (KC.at[CX], KC.at[0]),
            (KC.at[1], KC.at[CX + 1]),
            (KYS.at[0], KYR.at[0]),
            (KYS.at[1], KYR.at[1]),
            (KZS.at[0], KZR.at[0]),
            (KZS.at[1], KZR.at[1]),
        )[side]
        return pltpu.make_async_remote_copy(
            src_ref=src, dst_ref=dst, send_sem=k_ss.at[side], recv_sem=k_rs.at[side],
            device_id=sides[side], device_id_type=MESH,
        )

    def h_copy(step, side):
        inner = pl.ds(1, CY)
        src, dst = (
            (F.at[step, CX, inner], F.at[step, 0, inner]),
            (F.at[step, 1, inner], F.at[step, CX + 1, inner]),
            (YS.at[step, 0], YR.at[step, 0]),
            (YS.at[step, 1], YR.at[step, 1]),
            (ZS.at[step, 0], ZR.at[step, 0]),
            (ZS.at[step, 1], ZR.at[step, 1]),
        )[side]
        return pltpu.make_async_remote_copy(
            src_ref=src, dst_ref=dst, send_sem=h_ss.at[step, side], recv_sem=h_rs.at[step, side],
            device_id=sides[side], device_id_type=MESH,
        )

    def pz_copy(delta):
        slot = plan.z_slot_of_me_at(delta)
        return pltpu.make_async_remote_copy(
            src_ref=POSZ.at[plan.z_own], dst_ref=POSZ.at[slot], send_sem=pz_ss.at[slot], recv_sem=pz_rs.at[slot],
            device_id=plan.z_peer(delta), device_id_type=MESH,
        )

    def pp_copy(delta):
        slot = plan.p_slot_of_me_at(delta)
        return pltpu.make_async_remote_copy(
            src_ref=POSP.at[plan.p_own], dst_ref=POSP.at[slot], send_sem=pp_ss.at[slot], recv_sem=pp_rs.at[slot],
            device_id=plan.p_peer(delta), device_id_type=MESH,
        )

    def t_slot(it, slot):
        return TR.at[it, slot // 2, :, pl.ds((slot % 2) * ND, ND)]

    def t_copy(it, delta):
        slot = plan.z_slot_of_me_at(delta)
        return pltpu.make_async_remote_copy(
            src_ref=t_slot(it, plan.z_own), dst_ref=t_slot(it, slot), send_sem=t_ss.at[it, slot],
            recv_sem=t_rs.at[it, slot], device_id=plan.z_peer(delta), device_id_type=MESH,
        )

    def r_copy(it, slot):
        return pltpu.make_async_remote_copy(
            src_ref=ACC.at[it, slot], dst_ref=RR.at[it, slot], send_sem=r_ss.at[it, slot],
            recv_sem=r_rs.at[it, slot], device_id=plan.p_peer(plan.p_deltas[slot]), device_id_type=MESH,
        )

    y_first = (2, 3, 0, 1, 4, 5)
    far_first = sorted((d for d in plan.z_deltas if d), key=lambda d: -min(d, n_z - d))
    for side in y_first:
        k_copy(side).start()
    for delta in far_first:
        pz_copy(delta).start()
    for delta in plan.p_deltas:
        if delta != (0, 0):
            pp_copy(delta).start()

    def add_nodes(flux, scaled):
        hi = flux.astype(BF16).astype(F32)
        mid = (flux - hi).astype(BF16).astype(F32)
        low = (flux - hi) - mid

        def body(x, _):
            total = jnp.zeros((CY * E, CZ), F32)
            for part in (hi, mid, low):
                picked = [jnp.where(rows16 == x * CY + y, part, 0.0) for y in range(CY)]
                left = jnp.concatenate(picked, axis=0).astype(BF16)
                total = total + lax.dot_general(
                    left, OH[...], (((1,), (1,)), ((), ())), preferred_element_type=F32
                )
            for y in range(CY):
                b = S[x, y] + total[y * E : (y + 1) * E]
                if scaled:
                    b = b * DI[pl.ds(x * CY + y, 1), :]
                B[x, y] = b
            return 0

        lax.fori_loop(0, CX, body, 0)

    over_blocks(lambda x, y: source_copy(x, y).wait())
    add_nodes(incident[...], False)

    for side in range(6):
        k_copy(side).wait_recv()
    v, r, c = plan.v, plan.r, plan.c
    inside = [
        jnp.where(v == plan.n_vol - 1, 0.0, 1.0), jnp.where(v == 0, 0.0, 1.0),
        jnp.where(r == plan.n_row - 1, 0.0, 1.0), jnp.where(r == 0, 0.0, 1.0),
        jnp.where(c == plan.n_col - 1, 0.0, 1.0), jnp.where(c == 0, 0.0, 1.0),
    ]
    for x in range(CX):
        k = KC[x + 1]
        edge = [
            jnp.full((8, 128), x == CX - 1), jnp.full((8, 128), x == 0),
            subs == CY - 1, subs == 0, lanes == CZ - 1, lanes == 0,
        ]
        beyond = [
            KC[x + 2], KC[x],
            jnp.where(edge[2], jnp.broadcast_to(KYR[1, x : x + 1, :], (8, 128)), pltpu.roll(k, 7, 0)),
            jnp.where(edge[3], jnp.broadcast_to(KYR[0, x : x + 1, :], (8, 128)), pltpu.roll(k, 1, 0)),
            jnp.where(edge[4], pltpu.roll(KZR[1], 127 - x, 1), pltpu.roll(k, 127, 1)),
            jnp.where(edge[5], pltpu.roll(KZR[0], (128 - x) % 128, 1), pltpu.roll(k, 1, 1)),
        ]
        keep = []
        for side in range(6):
            if side >= 2 or (x == CX - 1 and side == 0) or (x == 0 and side == 1):
                keep.append(jnp.where(edge[side], inside[side], 1.0))
            else:
                keep.append(None)
        faces = []
        for side in range(6):
            other = beyond[side] if keep[side] is None else beyond[side] * keep[side]
            faces.append(0.5 * (k + other))
        diag = MASS_TERM + faces[0]
        for face in faces[1:]:
            diag = diag + face
        inverse = 1.0 / diag
        DI[x * CY : (x + 1) * CY, :] = inverse
        for side in range(6):
            face = faces[side] if keep[side] is None else faces[side] * keep[side]
            CO[side, x * CY : (x + 1) * CY, :] = face * inverse

    def pack(lane, value, down, up):
        here = lanes == lane
        down = jnp.where(here, pltpu.roll(value, lane, 1), down)
        up = jnp.where(here, pltpu.roll(value, lax.rem(lane + 1, 128), 1), up)
        return down, up

    def sweep(step):
        weight = weights[step]
        last = step == STEPS - 1
        if step > 0:
            for side in range(6):
                h_copy(step - 1, side).wait_recv()

            def spread(x, _):
                F[step - 1, x + 1, 0] = YR[step - 1, 0, x].astype(F32)
                F[step - 1, x + 1, CY + 1] = YR[step - 1, 1, x].astype(F32)
                return 0

            lax.fori_loop(0, CX, spread, 0)
            z_up, z_down = ZR[step - 1, 1], ZR[step - 1, 0]

        def body(x, carry):
            down, up = carry
            for y in range(CY):
                at = x * CY + y
                if step > 0:
                    co = [jnp.broadcast_to(CO[side, pl.ds(at, 1), :], (8, 128)) for side in range(6)]
                halves = []
                for h in range(2):
                    rows_h = pl.ds(8 * h, 8)
                    lane = x * 16 + (y * 2 + h)
                    if step == 0:
                        b = B[x, y, rows_h, :] * DI[pl.ds(at, 1), :]
                        B[x, y, rows_h, :] = b
                        new = weight * b
                    else:
                        value = F[step - 1, x + 1, y + 1, rows_h, :]
                        zp = jnp.where(
                            lanes == CZ - 1, pltpu.roll(z_up, 127 - lane, 1), pltpu.roll(value, 127, 1)
                        )
                        zm = jnp.where(
                            lanes == 0, pltpu.roll(z_down, lax.rem(128 - lane, 128), 1), pltpu.roll(value, 1, 1)
                        )
                        total = B[x, y, rows_h, :] + co[0] * F[step - 1, x + 2, y + 1, rows_h, :]
                        total = total + co[1] * F[step - 1, x, y + 1, rows_h, :]
                        total = total + co[2] * F[step - 1, x + 1, y + 2, rows_h, :]
                        total = total + co[3] * F[step - 1, x + 1, y, rows_h, :]
                        total = total + co[4] * zp
                        total = total + co[5] * zm
                        new = (1.0 - weight) * value + weight * total
                    F[step, x + 1, y + 1, rows_h, :] = new
                    if not last:
                        down, up = pack(lane, new, down, up)
                    halves.append(new)
                if not last and y in (0, CY - 1):
                    YS[step, 0 if y else 1, x] = jnp.concatenate(halves, axis=0).astype(BF16)
            return down, up

        zero = jnp.zeros((8, 128), F32)
        down, up = lax.fori_loop(0, CX, body, (zero, zero))
        if not last:
            ZS[step, 0] = up
            ZS[step, 1] = down

    def send_halos(step):
        for side in y_first:
            h_copy(step, side).start()

    g_steps = n_z * (ND // 16)

    def spread_positions():
        for delta in far_first:
            pz_copy(delta).wait_recv()
        for delta in plan.p_deltas:
            if delta != (0, 0):
                pp_copy(delta).wait_recv()

        def body(slot, _):
            wide = jnp.concatenate([POSZ[slot]] * 16, axis=0).T
            for axis in range(3):
                PJ[slot, axis] = jnp.broadcast_to(wide[:, axis : axis + 1], (ND, 128))
            return 0

        lax.fori_loop(0, n_z, body, 0)

    soft = SOFTENING * SOFTENING * inverse_scale * inverse_scale

    def build(first, past):
        def body(t, _):
            slot, group = lax.div(t, 8), lax.rem(t, 8)
            q, half = lax.div(slot, 2), lax.rem(slot, 2)
            mine = [PJ[slot, axis, pl.ds(group * 16, 16), :] for axis in range(3)]
            for n in range(n_p):
                dx, dy, dz = (
                    mine[axis] - jnp.broadcast_to(POSP[n, axis : axis + 1, :], (16, 128)) for axis in range(3)
                )
                squared = dx * dx + dy * dy + dz * dz
                tile = lax.rsqrt(squared + soft).astype(BF16)
                G[q, n // 2, pl.ds(half * ND + group * 16, 16), (n % 2) * ND : (n % 2 + 1) * ND] = tile
            return 0

        lax.fori_loop(first, past, body, 0)

    def read_traces(it, step):
        def body(x, acc):
            block = F[step, x + 1, pl.ds(1, CY)].reshape(CY * E, CZ).astype(BF16)
            at_nodes = jnp.dot(block, OH[...], preferred_element_type=F32)
            for y in range(CY):
                acc = jnp.where(rows16 == x * CY + y, at_nodes[y * E : (y + 1) * E], acc)
            return acc

        traces = lax.fori_loop(0, CX, body, jnp.zeros((E, ND), F32))
        own = plan.z_own
        TR[it, own // 2, :, (own % 2) * ND : (own % 2 + 1) * ND] = traces.astype(BF16)
        for delta in far_first:
            t_copy(it, delta).start()

    def product(it):
        for q in range(n_q):
            for slot in (2 * q, 2 * q + 1):
                if slot != plan.z_own:
                    delta = (n_z - plan.z_deltas[slot]) % n_z
                    t_copy(it, delta).wait_recv()
            left = TR[it, q]

            def tile(m, fresh=(q == 0), q=q, left=left):
                part = jnp.dot(left, G[q, m], preferred_element_type=F32)
                for side in range(2):
                    block = part[:, side * ND : (side + 1) * ND]
                    if fresh:
                        ACC[it, 2 * m + side] = block
                    else:
                        ACC[it, 2 * m + side] += block

            if q < n_q - 1:
                def body(m, _, tile=tile):
                    tile(m)
                    return 0

                lax.fori_loop(0, n_m, body, 0)
            else:
                for m in range(n_m):
                    tile(m)
                    for slot in (2 * m, 2 * m + 1):
                        if slot != plan.p_own:
                            r_copy(it, slot).start()
        total = ACC[it, plan.p_own]
        for slot in range(n_p):
            if slot != plan.p_own:
                r_copy(it, slot).wait_recv()
                total = total + RR[it, slot]
        return incident[...] + total

    sweep(0)
    send_halos(0)
    spread_positions()
    chunk = g_steps // (SWEEPS - 1)
    bounds = [0, chunk, 2 * chunk, g_steps]
    flux = None
    for it in range(ITERS):
        base = it * SWEEPS
        if it > 0:
            add_nodes(flux, True)
        for s in range(SWEEPS):
            step = base + s
            if step > 0:
                sweep(step)
                if s < SWEEPS - 1:
                    send_halos(step)
            if it == 0 and s < SWEEPS - 1:
                build(bounds[s], bounds[s + 1])
        read_traces(it, base + SWEEPS - 1)
        if it < ITERS - 1:
            send_halos(base + SWEEPS - 1)
        else:
            over_blocks(lambda x, y: field_copy(x, y).start())
        flux = product(it)
    flux_out[...] = flux

    over_blocks(lambda x, y: field_copy(x, y).wait())
    for side in range(6):
        k_copy(side).wait_send()
        for step in range(HALOS):
            h_copy(step, side).wait_send()
    for delta in far_first:
        pz_copy(delta).wait_send()
        for it in range(ITERS):
            t_copy(it, delta).wait_send()
    for slot, delta in enumerate(plan.p_deltas):
        if delta != (0, 0):
            pp_copy(delta).wait_send()
            for it in range(ITERS):
                r_copy(it, slot).wait_send()


def solution(mesh):
    plan = Plan(mesh)
    vmem = pl.BlockSpec(memory_space=pltpu.VMEM)
    smem = pl.BlockSpec(memory_space=pltpu.SMEM)
    hbm = pl.BlockSpec(memory_space=pl.ANY)
    dma = pltpu.SemaphoreType.DMA

    def per_device(source, labels, region_coeff, node_cell, node_pos, incident):
        return pl.pallas_call(
            functools.partial(kernel, plan),
            out_shape=(
                jax.ShapeDtypeStruct((E, CX, CY, CZ), F32),
                jax.ShapeDtypeStruct((E, ND), F32),
            ),
            in_specs=[hbm, vmem, smem, vmem, vmem, vmem],
            out_specs=(hbm, vmem),
            scratch_shapes=[
                pltpu.VMEM((STEPS, CX + 2, CY + 2, E, CZ), F32),
                pltpu.VMEM((CX, CY, E, CZ), F32),
                pltpu.VMEM((CX, CY, E, CZ), F32),
                pltpu.VMEM((CX + 2, CY, CZ), F32),
                pltpu.VMEM((2, CX, CZ), F32),
                pltpu.VMEM((2, CX, CZ), F32),
                pltpu.VMEM((2, 8, 128), F32),
                pltpu.VMEM((2, 8, 128), F32),
                pltpu.VMEM((6, CX * CY, CZ), F32),
                pltpu.VMEM((CX * CY, CZ), F32),
                pltpu.VMEM((HALOS, 2, CX, E, CZ), BF16),
                pltpu.VMEM((HALOS, 2, CX, E, CZ), BF16),
                pltpu.VMEM((HALOS, 2, 8, 128), F32),
                pltpu.VMEM((HALOS, 2, 8, 128), F32),
                pltpu.VMEM((CZ, ND), BF16),
                pltpu.VMEM((ITERS, plan.n_q, E, 2 * ND), BF16),
                pltpu.VMEM((ITERS, plan.n_p, E, ND), F32),
                pltpu.VMEM((ITERS, plan.n_p, E, ND), F32),
                pltpu.VMEM((plan.n_q, plan.n_m, 2 * ND, 2 * ND), BF16),
                pltpu.VMEM((plan.n_z, 8, ND), F32),
                pltpu.VMEM((plan.n_p, 8, ND), F32),
                pltpu.VMEM((plan.n_z, 3, ND, 128), F32),
                dma,
                dma,
                dma((6,)),
                dma((6,)),
                dma((HALOS, 6)),
                dma((HALOS, 6)),
                dma((plan.n_z,)),
                dma((plan.n_z,)),
                dma((plan.n_p,)),
                dma((plan.n_p,)),
                dma((ITERS, plan.n_z)),
                dma((ITERS, plan.n_z)),
                dma((ITERS, plan.n_p)),
                dma((ITERS, plan.n_p)),
            ],
            compiler_params=pltpu.CompilerParams(collective_id=0, has_side_effects=True),
            name="coupled",
        )(source, labels, region_coeff, node_cell.reshape(1, ND), node_pos, incident)

    placed = (
        P(None, "vol", "row", "col"),
        P("vol", "row", "col"),
        P(),
        P(("vol", "row", "col")),
        P(None, ("vol", "row", "col")),
        P(None, ("vol", "row", "col")),
    )
    return jax.shard_map(
        per_device,
        mesh=mesh,
        in_specs=placed,
        out_specs=(P(None, "vol", "row", "col"), P(None, ("vol", "row", "col"))),
        check_vma=False,
    )
```

time: 1830 us -> 143 us (0.08)
  blocking collectives: 1310 us -> 0 us
  starting transfers between devices: 214 us -> 0 us
  Pallas kernels: 0 us -> 140 us
  waiting for transfers between devices: 121 us -> 0 us
  local copies, waits for them, and re-layouts: 86.2 us -> 2.49 us
  other arithmetic: 64.6 us -> 0 us
    all_gather x4 -> x0, blocking collectives: 1310 us -> none  [the longest x2 887 us: per_device(): lax.all_gather(traces, ('vol', 'row'), axis=1, tiled=True)]
    ppermute x54 -> x0, starting transfers between devices: 214 us -> none  [the longest x27 133 us: padded_2(): lax.ppermute(tail, axis, [(i, (i + 1) % count) for i in range(ends)])]
    pallas_call x0 -> x1, Pallas kernels: none -> 140 us  [per_device(): pl.pallas_call(functools.partial(kernel, plan), out_shape=(jax.ShapeDtype...]
    reduce_scatter x2 -> x0, waiting for transfers between devices: 67.5 us -> none  [per_device(): lax.psum_scatter(partial_flux, 'col', scatter_dimension=1, tiled=True)]
    ppermute x54 -> x0, waiting for transfers between devices: 53.3 us -> none  [the longest x27 26.7 us: padded_2(): lax.ppermute(head, axis, [((i + 1) % count, i) for i in range(ends)])]
    slice x66 -> x0, local copies, waits for them, and re-layouts: 37.2 us -> none  [the longest x32 15.7 us: one_block(): delta_x = point_block[0][:, None] - row_pos[0][None, :]]
    convert_element_type x16 -> x0, other arithmetic: 30.3 us -> none  [one_block(): (scale * lax.rsqrt(squared + SOFTENING * SOFTENING)).astype(jnp.bfloat16)]
    ppermute x16 -> x0, local copies, waits for them, and re-layouts: 19.5 us -> none  [the longest x8 11.1 us: padded_2(): lax.ppermute(head, axis, [((i + 1) % count, i) for i in range(ends)])]
  transfers between devices with their start and end apart: 56 -> 0, of which waited for: 25 -> 0; matrix products, arithmetic and copies ran while one was open for 4% -> 0% of each run, Pallas kernels for 0% -> 0%
where the time goes in v1:
time: 143 us
  Pallas kernels  140 us (98%)
  local copies, waits for them, and re-layouts  2.49 us (2%)
    pallas_call x1, Pallas kernels, per_device(): pl.pallas_call(functools.partial(kernel, plan), out_shape=(jax.ShapeDtype...  140 us

profile of v1, /device:TPU:1, one launch (start us, length us, event | category | flops | bytes accessed | tf_op | source)
XLA Modules:
  0.0 142.6 jit_solution(10654219539960192744)
XLA Ops:
  0.6 139.5 %coupled.1 = (f32[16,8,8,128]{3,2,1,0:T(8,128)}, f32[16,128]{1,0:T(8,128)}) custom-call(f32[16,8,8,128]{3,2,1,0:T(8,128)} %source.1, s32[8,8,128]{2,1,0:T(8,128)} %labels.1, f32[8]{0:T(128)} %coeff.1, s32[1,128]{1,0:T(1,128)} %bitcast.1, f32[3,128]{1,0:T(4,128)} %pos.1, f32[16,128]{1,0:T(8,128)} %incident.1), custom_call_target="tpu_custom_call" | custom-call | tf_op jit(solution)/shard_map/coupled/pallas_call | solution.py:497
  140.1 0.0 copy-start
  140.2 1.9 %copy.10 = f32[16,8,8,128]{3,2,1,0:T(8,128)} copy(f32[16,8,8,128]{3,2,1,0:T(8,128)} %get-tuple-element.4) | data formatting | bytes 1048576
  142.0 0.0 copy-done
  142.1 0.6 copy.11
Async XLA Ops:
  140.1 1.9 %copy-start = (f32[16,128]{1,0:T(8,128)S(1)}, f32[16,128]{1,0:T(8,128)}, u32[]{:S(2)}) copy-start(f32[16,128]{1,0:T(8,128)} %get-tuple-element.5) | copy-start | bytes 24580

commit v2 on v1

--- a/solution.py
+++ b/solution.py
@@ -22,6 +22,7 @@
 E, CX, CY, CZ, ND = 16, 8, 8, 128, 128
 STEPS = SWEEPS * ITERS
 HALOS = STEPS - 1
+EDGE_GROUP, INNER_GROUP = 4, 2
 
 
 def sweep_weights(count):
@@ -96,7 +97,7 @@
 def kernel(
     plan, source, labels, coeff, cell, pos, incident, field_out, flux_out,
     F, S, B, KC, KYS, KYR, KZS, KZR, CO, DI, YS, YR, ZS, ZR, OH, TR, ACC, RR, G, POSZ, POSP, PJ,
-    src_sem, out_sem, k_ss, k_rs, h_ss, h_rs, pz_ss, pz_rs, pp_ss, pp_rs, t_ss, t_rs, r_ss, r_rs,
+    src_sem, k_ss, k_rs, h_ss, h_rs, pz_ss, pz_rs, pp_ss, pp_rs, t_ss, t_rs, r_ss, r_rs,
 ):
     plan.here()
     weights = sweep_weights(SWEEPS) * ITERS
@@ -107,9 +108,6 @@
 
     def source_copy(x, y):
         return pltpu.make_async_copy(source.at[:, x, y, :], S.at[x, y], src_sem)
-
-    def field_copy(x, y):
-        return pltpu.make_async_copy(F.at[STEPS - 1, x + 1, y + 1], field_out.at[:, x, y, :], out_sem)
 
     def over_blocks(act):
         def body(x, _):
@@ -144,9 +142,9 @@
     KZS[1] = kz_down
 
     inverse_scale = math.sqrt(plan.nodes) / KERNEL_GAIN
-    own_pos = jnp.concatenate([pos[...] * inverse_scale, jnp.zeros((5, 128), F32)], axis=0)
-    POSZ[plan.z_own] = own_pos
-    POSP[plan.p_own] = own_pos
+    own_pos = pos[...] * inverse_scale
+    POSZ[plan.z_own, 0:3, :] = own_pos
+    POSP[plan.p_own, 0:3, :] = own_pos
     cells = jnp.broadcast_to(cell[...], (8, 128))
     rows = lax.div(cells, CZ)
     rows16 = jnp.concatenate([rows, rows], axis=0)
@@ -189,14 +187,14 @@
     def pz_copy(delta):
         slot = plan.z_slot_of_me_at(delta)
         return pltpu.make_async_remote_copy(
-            src_ref=POSZ.at[plan.z_own], dst_ref=POSZ.at[slot], send_sem=pz_ss.at[slot], recv_sem=pz_rs.at[slot],
+            src_ref=POSZ.at[plan.z_own, pl.ds(0, 3)], dst_ref=POSZ.at[slot, pl.ds(0, 3)], send_sem=pz_ss.at[slot], recv_sem=pz_rs.at[slot],
             device_id=plan.z_peer(delta), device_id_type=MESH,
         )
 
     def pp_copy(delta):
         slot = plan.p_slot_of_me_at(delta)
         return pltpu.make_async_remote_copy(
-            src_ref=POSP.at[plan.p_own], dst_ref=POSP.at[slot], send_sem=pp_ss.at[slot], recv_sem=pp_rs.at[slot],
+            src_ref=POSP.at[plan.p_own, pl.ds(0, 3)], dst_ref=POSP.at[slot, pl.ds(0, 3)], send_sem=pp_ss.at[slot], recv_sem=pp_rs.at[slot],
             device_id=plan.p_peer(delta), device_id_type=MESH,
         )
 
@@ -216,24 +214,35 @@
             recv_sem=r_rs.at[it, slot], device_id=plan.p_peer(plan.p_deltas[slot]), device_id_type=MESH,
         )
 
+    flights = {}
+
+    def launch(copy, *key):
+        flight = copy(*key)
+        flight.start()
+        flights[(copy, *key)] = [flight, False]
+
+    def arrive(copy, *key):
+        entry = flights[(copy, *key)]
+        entry[0].wait_recv()
+        entry[1] = True
+
     y_first = (2, 3, 0, 1, 4, 5)
     far_first = sorted((d for d in plan.z_deltas if d), key=lambda d: -min(d, n_z - d))
     for side in y_first:
-        k_copy(side).start()
+        launch(k_copy, side)
     for delta in far_first:
-        pz_copy(delta).start()
+        launch(pz_copy, delta)
     for delta in plan.p_deltas:
         if delta != (0, 0):
-            pp_copy(delta).start()
+            launch(pp_copy, delta)
 
     def add_nodes(flux, scaled):
         hi = flux.astype(BF16).astype(F32)
-        mid = (flux - hi).astype(BF16).astype(F32)
-        low = (flux - hi) - mid
+        low = flux - hi
 
         def body(x, _):
             total = jnp.zeros((CY * E, CZ), F32)
-            for part in (hi, mid, low):
+            for part in (hi, low):
                 picked = [jnp.where(rows16 == x * CY + y, part, 0.0) for y in range(CY)]
                 left = jnp.concatenate(picked, axis=0).astype(BF16)
                 total = total + lax.dot_general(
@@ -246,13 +255,46 @@
                 B[x, y] = b
             return 0
 
-        lax.fori_loop(0, CX, body, 0)
+        lax.fori_loop(0, CX, body, 0, unroll=True)
+
+    soft = SOFTENING * SOFTENING * inverse_scale * inverse_scale
+
+    def build(first, past):
+        for slot in range(first // 8, (past + 7) // 8):
+            if slot * 8 >= first:
+                if slot != plan.z_own:
+                    arrive(pz_copy, (n_z - plan.z_deltas[slot]) % n_z)
+                columns = POSZ[slot]
+                wide = jnp.concatenate([columns] * 16, axis=0).T
+                for axis in range(3):
+                    PJ[slot, axis] = jnp.broadcast_to(wide[:, axis : axis + 1], (ND, 128))
+
+        def body(t, _):
+            slot, group = lax.div(t, 8), lax.rem(t, 8)
+            q, half = lax.div(slot, 2), lax.rem(slot, 2)
+            mine = [PJ[slot, axis, pl.ds(group * 16, 16), :] for axis in range(3)]
+            for n in range(n_p):
+                dx, dy, dz = (
+                    mine[axis] - jnp.broadcast_to(POSP[n, axis : axis + 1, :], (16, 128)) for axis in range(3)
+                )
+                squared = dx * dx + dy * dy + dz * dz
+                tile = lax.rsqrt(squared + soft).astype(BF16)
+                G[q, n // 2, pl.ds(half * ND + group * 16, 16), (n % 2) * ND : (n % 2 + 1) * ND] = tile
+            return 0
+
+        lax.fori_loop(first, past, body, 0)
 
     over_blocks(lambda x, y: source_copy(x, y).wait())
     add_nodes(incident[...], False)
+    for delta in plan.p_deltas:
+        if delta != (0, 0):
+            arrive(pp_copy, delta)
+    g_steps = n_z * (ND // 16)
+    bounds = [g_steps * part // 16 for part in (2, 5, 9, 12)]
+    build(0, bounds[0])
 
     for side in range(6):
-        k_copy(side).wait_recv()
+        arrive(k_copy, side)
     v, r, c = plan.v, plan.r, plan.c
     inside = [
         jnp.where(v == plan.n_vol - 1, 0.0, 1.0), jnp.where(v == 0, 0.0, 1.0),
@@ -291,18 +333,16 @@
             face = faces[side] if keep[side] is None else faces[side] * keep[side]
             CO[side, x * CY : (x + 1) * CY, :] = face * inverse
 
-    def pack(lane, value, down, up):
-        here = lanes == lane
-        down = jnp.where(here, pltpu.roll(value, lane, 1), down)
-        up = jnp.where(here, pltpu.roll(value, lax.rem(lane + 1, 128), 1), up)
-        return down, up
-
-    def sweep(step):
+    def turn(value, lanes_up):
+        return pltpu.roll(value, lanes_up % 128, 1) if lanes_up % 128 else value
+
+    def sweep(step, hold=False):
         weight = weights[step]
         last = step == STEPS - 1
+        zero = jnp.zeros((8, 128), F32)
         if step > 0:
             for side in range(6):
-                h_copy(step - 1, side).wait_recv()
+                arrive(h_copy, step - 1, side)
 
             def spread(x, _):
                 F[step - 1, x + 1, 0] = YR[step - 1, 0, x].astype(F32)
@@ -310,145 +350,110 @@
                 return 0
 
             lax.fori_loop(0, CX, spread, 0)
-            z_up, z_down = ZR[step - 1, 1], ZR[step - 1, 0]
-
-        def body(x, carry):
-            down, up = carry
-            for y in range(CY):
-                at = x * CY + y
-                if step > 0:
-                    co = [jnp.broadcast_to(CO[side, pl.ds(at, 1), :], (8, 128)) for side in range(6)]
-                halves = []
-                for h in range(2):
-                    rows_h = pl.ds(8 * h, 8)
-                    lane = x * 16 + (y * 2 + h)
-                    if step == 0:
-                        b = B[x, y, rows_h, :] * DI[pl.ds(at, 1), :]
-                        B[x, y, rows_h, :] = b
-                        new = weight * b
-                    else:
-                        value = F[step - 1, x + 1, y + 1, rows_h, :]
-                        zp = jnp.where(
-                            lanes == CZ - 1, pltpu.roll(z_up, 127 - lane, 1), pltpu.roll(value, 127, 1)
-                        )
-                        zm = jnp.where(
-                            lanes == 0, pltpu.roll(z_down, lax.rem(128 - lane, 128), 1), pltpu.roll(value, 1, 1)
-                        )
-                        total = B[x, y, rows_h, :] + co[0] * F[step - 1, x + 2, y + 1, rows_h, :]
-                        total = total + co[1] * F[step - 1, x, y + 1, rows_h, :]
-                        total = total + co[2] * F[step - 1, x + 1, y + 2, rows_h, :]
-                        total = total + co[3] * F[step - 1, x + 1, y, rows_h, :]
-                        total = total + co[4] * zp
-                        total = total + co[5] * zm
-                        new = (1.0 - weight) * value + weight * total
-                    F[step, x + 1, y + 1, rows_h, :] = new
-                    if not last:
-                        down, up = pack(lane, new, down, up)
-                    halves.append(new)
-                if not last and y in (0, CY - 1):
-                    YS[step, 0 if y else 1, x] = jnp.concatenate(halves, axis=0).astype(BF16)
-            return down, up
-
-        zero = jnp.zeros((8, 128), F32)
-        down, up = lax.fori_loop(0, CX, body, (zero, zero))
+
+        def body(i, carry, ys, group):
+            down, up, z_up, z_down = carry
+            for u in range(group):
+                x = i * group + u
+                for y in ys:
+                    at = x * CY + y
+                    if step > 0:
+                        co = [jnp.broadcast_to(CO[side, pl.ds(at, 1), :], (8, 128)) for side in range(6)]
+                    halves = []
+                    for h in range(2):
+                        rows_h = pl.ds(8 * h, 8)
+                        local = u * 16 + y * 2 + h
+                        if step == 0:
+                            b = B[x, y, rows_h, :] * DI[pl.ds(at, 1), :]
+                            B[x, y, rows_h, :] = b
+                            new = weight * b
+                        else:
+                            value = F[step - 1, x + 1, y + 1, rows_h, :]
+                            zp = jnp.where(lanes == CZ - 1, turn(z_up, 127 - local), turn(value, 127))
+                            zm = jnp.where(lanes == 0, turn(z_down, 129 - local), turn(value, 1))
+                            total = B[x, y, rows_h, :] + co[0] * F[step - 1, x + 2, y + 1, rows_h, :]
+                            total = total + co[1] * F[step - 1, x, y + 1, rows_h, :]
+                            total = total + co[2] * F[step - 1, x + 1, y + 2, rows_h, :]
+                            total = total + co[3] * F[step - 1, x + 1, y, rows_h, :]
+                            total = total + co[4] * zp
+                            total = total + co[5] * zm
+                            new = (1.0 - weight) * value + weight * total
+                        if last:
+                            field_out[x, y, rows_h, :] = new
+                        else:
+                            F[step, x + 1, y + 1, rows_h, :] = new
+                            lane = i * (16 * group) + local
+                            turned = pltpu.roll(new, lane, 1)
+                            down = jnp.where(lanes == lane, turned, down)
+                            up = jnp.where(lanes == (lane + 127) % 128, turned, up)
+                        halves.append(new)
+                    if not last and y in (0, CY - 1):
+                        YS[step, 0 if y else 1, x] = jnp.concatenate(halves, axis=0).astype(BF16)
+            if step > 0:
+                z_up, z_down = turn(z_up, -16 * group), turn(z_down, -16 * group)
+            return down, up, z_up, z_down
+
+        def every(ys, group, carry):
+            return lax.fori_loop(0, CX // group, functools.partial(body, ys=ys, group=group), carry)
+
+        beyond_z = (ZR[step - 1, 1], ZR[step - 1, 0]) if step > 0 else (zero, zero)
+        carry = every((0, CY - 1), EDGE_GROUP, (zero, zero) + beyond_z)
+        if not last and not hold:
+            for side in (2, 3):
+                launch(h_copy, step, side)
+        down, up, _, _ = every(range(1, CY - 1), INNER_GROUP, carry)
         if not last:
             ZS[step, 0] = up
             ZS[step, 1] = down
+            if not hold:
+                for side in (0, 1, 4, 5):
+                    launch(h_copy, step, side)
 
     def send_halos(step):
         for side in y_first:
-            h_copy(step, side).start()
-
-    g_steps = n_z * (ND // 16)
-
-    def spread_positions():
-        for delta in far_first:
-            pz_copy(delta).wait_recv()
-        for delta in plan.p_deltas:
-            if delta != (0, 0):
-                pp_copy(delta).wait_recv()
-
-        def body(slot, _):
-            wide = jnp.concatenate([POSZ[slot]] * 16, axis=0).T
-            for axis in range(3):
-                PJ[slot, axis] = jnp.broadcast_to(wide[:, axis : axis + 1], (ND, 128))
-            return 0
-
-        lax.fori_loop(0, n_z, body, 0)
-
-    soft = SOFTENING * SOFTENING * inverse_scale * inverse_scale
-
-    def build(first, past):
-        def body(t, _):
-            slot, group = lax.div(t, 8), lax.rem(t, 8)
-            q, half = lax.div(slot, 2), lax.rem(slot, 2)
-            mine = [PJ[slot, axis, pl.ds(group * 16, 16), :] for axis in range(3)]
-            for n in range(n_p):
-                dx, dy, dz = (
-                    mine[axis] - jnp.broadcast_to(POSP[n, axis : axis + 1, :], (16, 128)) for axis in range(3)
-                )
-                squared = dx * dx + dy * dy + dz * dz
-                tile = lax.rsqrt(squared + soft).astype(BF16)
-                G[q, n // 2, pl.ds(half * ND + group * 16, 16), (n % 2) * ND : (n % 2 + 1) * ND] = tile
-            return 0
-
-        lax.fori_loop(first, past, body, 0)
+            launch(h_copy, step, side)
 
     def read_traces(it, step):
         def body(x, acc):
-            block = F[step, x + 1, pl.ds(1, CY)].reshape(CY * E, CZ).astype(BF16)
+            block = field_out[x] if step == STEPS - 1 else F[step, x + 1, pl.ds(1, CY)]
+            block = block.reshape(CY * E, CZ).astype(BF16)
             at_nodes = jnp.dot(block, OH[...], preferred_element_type=F32)
             for y in range(CY):
                 acc = jnp.where(rows16 == x * CY + y, at_nodes[y * E : (y + 1) * E], acc)
             return acc
 
-        traces = lax.fori_loop(0, CX, body, jnp.zeros((E, ND), F32))
+        traces = lax.fori_loop(0, CX, body, jnp.zeros((E, ND), F32), unroll=True)
         own = plan.z_own
         TR[it, own // 2, :, (own % 2) * ND : (own % 2 + 1) * ND] = traces.astype(BF16)
         for delta in far_first:
-            t_copy(it, delta).start()
+            launch(t_copy, it, delta)
 
     def product(it):
         for q in range(n_q):
             for slot in (2 * q, 2 * q + 1):
                 if slot != plan.z_own:
                     delta = (n_z - plan.z_deltas[slot]) % n_z
-                    t_copy(it, delta).wait_recv()
+                    arrive(t_copy, it, delta)
             left = TR[it, q]
 
-            def tile(m, fresh=(q == 0), q=q, left=left):
+            for m in range(n_m):
                 part = jnp.dot(left, G[q, m], preferred_element_type=F32)
                 for side in range(2):
                     block = part[:, side * ND : (side + 1) * ND]
-                    if fresh:
+                    if q == 0:
                         ACC[it, 2 * m + side] = block
                     else:
                         ACC[it, 2 * m + side] += block
-
-            if q < n_q - 1:
-                def body(m, _, tile=tile):
-                    tile(m)
-                    return 0
-
-                lax.fori_loop(0, n_m, body, 0)
-            else:
-                for m in range(n_m):
-                    tile(m)
-                    for slot in (2 * m, 2 * m + 1):
-                        if slot != plan.p_own:
-                            r_copy(it, slot).start()
+                    if q == n_q - 1 and 2 * m + side != plan.p_own:
+                        launch(r_copy, it, 2 * m + side)
         total = ACC[it, plan.p_own]
         for slot in range(n_p):
             if slot != plan.p_own:
-                r_copy(it, slot).wait_recv()
+                arrive(r_copy, it, slot)
                 total = total + RR[it, slot]
         return incident[...] + total
 
     sweep(0)
-    send_halos(0)
-    spread_positions()
-    chunk = g_steps // (SWEEPS - 1)
-    bounds = [0, chunk, 2 * chunk, g_steps]
     flux = None
     for it in range(ITERS):
         base = it * SWEEPS
@@ -457,33 +462,35 @@
         for s in range(SWEEPS):
             step = base + s
             if step > 0:
-                sweep(step)
-                if s < SWEEPS - 1:
-                    send_halos(step)
+                sweep(step, hold=s == SWEEPS - 1)
             if it == 0 and s < SWEEPS - 1:
                 build(bounds[s], bounds[s + 1])
         read_traces(it, base + SWEEPS - 1)
         if it < ITERS - 1:
             send_halos(base + SWEEPS - 1)
-        else:
-            over_blocks(lambda x, y: field_copy(x, y).start())
+            build(bounds[-1], g_steps)
         flux = product(it)
     flux_out[...] = flux
 
-    over_blocks(lambda x, y: field_copy(x, y).wait())
-    for side in range(6):
-        k_copy(side).wait_send()
-        for step in range(HALOS):
-            h_copy(step, side).wait_send()
-    for delta in far_first:
-        pz_copy(delta).wait_send()
-        for it in range(ITERS):
-            t_copy(it, delta).wait_send()
-    for slot, delta in enumerate(plan.p_deltas):
-        if delta != (0, 0):
-            pp_copy(delta).wait_send()
-            for it in range(ITERS):
-                r_copy(it, slot).wait_send()
+    for flight, arrived in flights.values():
+        if not arrived:
+            flight.wait_recv()
+        flight.wait_send()
+
+
+def write_out(field, flux, field_out, flux_out, field_sem, flux_sem):
+    flux_copy = pltpu.make_async_copy(flux, flux_out, flux_sem)
+    flux_copy.start()
+    copies = [
+        pltpu.make_async_copy(field.at[x, y], field_out.at[:, x, y, :], field_sem)
+        for x in range(CX)
+        for y in range(CY)
+    ]
+    for copy in copies:
+        copy.start()
+    for copy in copies:
+        copy.wait()
+    flux_copy.wait()
 
 
 def solution(mesh):
@@ -494,16 +501,16 @@
     dma = pltpu.SemaphoreType.DMA
 
     def per_device(source, labels, region_coeff, node_cell, node_pos, incident):
-        return pl.pallas_call(
+        field, flux = pl.pallas_call(
             functools.partial(kernel, plan),
             out_shape=(
-                jax.ShapeDtypeStruct((E, CX, CY, CZ), F32),
+                jax.ShapeDtypeStruct((CX, CY, E, CZ), F32),
                 jax.ShapeDtypeStruct((E, ND), F32),
             ),
             in_specs=[hbm, vmem, smem, vmem, vmem, vmem],
-            out_specs=(hbm, vmem),
+            out_specs=(vmem, vmem),
             scratch_shapes=[
-                pltpu.VMEM((STEPS, CX + 2, CY + 2, E, CZ), F32),
+                pltpu.VMEM((HALOS, CX + 2, CY + 2, E, CZ), F32),
                 pltpu.VMEM((CX, CY, E, CZ), F32),
                 pltpu.VMEM((CX, CY, E, CZ), F32),
                 pltpu.VMEM((CX + 2, CY, CZ), F32),
@@ -526,7 +533,6 @@
                 pltpu.VMEM((plan.n_p, 8, ND), F32),
                 pltpu.VMEM((plan.n_z, 3, ND, 128), F32),
                 dma,
-                dma,
                 dma((6,)),
                 dma((6,)),
                 dma((HALOS, 6)),
@@ -543,6 +549,17 @@
             compiler_params=pltpu.CompilerParams(collective_id=0, has_side_effects=True),
             name="coupled",
         )(source, labels, region_coeff, node_cell.reshape(1, ND), node_pos, incident)
+        return pl.pallas_call(
+            write_out,
+            out_shape=(
+                jax.ShapeDtypeStruct((E, CX, CY, CZ), F32),
+                jax.ShapeDtypeStruct((E, ND), F32),
+            ),
+            in_specs=[vmem, vmem],
+            out_specs=(hbm, hbm),
+            scratch_shapes=[dma, dma],
+            name="write_out",
+        )(field, flux)
 
     placed = (
         P(None, "vol", "row", "col"),

time: 143 us -> 105 us (0.73)
  Pallas kernels: 140 us -> 104 us
  local copies, waits for them, and re-layouts: 2.49 us -> 0 us
    pallas_call x1, Pallas kernels: 140 us -> 102 us  [per_device(): pl.pallas_call(functools.partial(kernel, plan), out_shape=(jax.ShapeDtype...]
    unnamed x4 -> x0, local copies, waits for them, and re-layouts: 2.49 us -> none
    pallas_call x0 -> x1, Pallas kernels: none -> 1.9 us  [per_device(): pl.pallas_call(write_out, out_shape=(jax.ShapeDtypeStruct((E, CX, CY, CZ)...]
where the time goes in v2:
time: 105 us
  Pallas kernels  104 us (99%)
    pallas_call x1, Pallas kernels, per_device(): pl.pallas_call(functools.partial(kernel, plan), out_shape=(jax.ShapeDtype...  102 us

profile of v2, /device:TPU:1, one launch (start us, length us, event | category | flops | bytes accessed | tf_op | source)
XLA Modules:
  0.0 104.9 jit_solution(11561006593124433743)
XLA Ops:
  0.6 102.2 %coupled.1 = (f32[8,8,16,128]{3,2,1,0:T(8,128)}, f32[16,128]{1,0:T(8,128)}) custom-call(f32[16,8,8,128]{3,2,1,0:T(8,128)} %source.1, s32[8,8,128]{2,1,0:T(8,128)} %labels.1, f32[8]{0:T(128)} %coeff.1, s32[1,128]{1,0:T(1,128)} %bitcast.1, f32[3,128]{1,0:T(4,128)} %pos.1, f32[16,128]{1,0:T(8,128)} %incident.1), custom_call_target="tpu_custom_call" | custom-call | tf_op jit(solution)/shard_map/coupled/pallas_call | solution.py:504
  102.8 1.9 %write_out.1 = (f32[16,8,8,128]{3,2,1,0:T(8,128)}, f32[16,128]{1,0:T(8,128)}) custom-call(f32[8,8,16,128]{3,2,1,0:T(8,128)} %get-tuple-element.4.field, f32[16,128]{1,0:T(8,128)} %get-tuple-element.5.flux), custom_call_target="tpu_custom_call" | custom-call | tf_op jit(solution)/shard_map/write_out/pallas_call | solution.py:552

commit v3 on v2

--- a/solution.py
+++ b/solution.py
@@ -286,12 +286,6 @@
 
     over_blocks(lambda x, y: source_copy(x, y).wait())
     add_nodes(incident[...], False)
-    for delta in plan.p_deltas:
-        if delta != (0, 0):
-            arrive(pp_copy, delta)
-    g_steps = n_z * (ND // 16)
-    bounds = [g_steps * part // 16 for part in (2, 5, 9, 12)]
-    build(0, bounds[0])
 
     for side in range(6):
         arrive(k_copy, side)
@@ -454,6 +448,11 @@
         return incident[...] + total
 
     sweep(0)
+    for delta in plan.p_deltas:
+        if delta != (0, 0):
+            arrive(pp_copy, delta)
+    g_steps = n_z * (ND // 16)
+    bounds = [g_steps * part // 16 for part in (0, 4, 8, 12)]
     flux = None
     for it in range(ITERS):
         base = it * SWEEPS
@@ -467,8 +466,8 @@
                 build(bounds[s], bounds[s + 1])
         read_traces(it, base + SWEEPS - 1)
         if it < ITERS - 1:
+            build(bounds[-1], g_steps)
             send_halos(base + SWEEPS - 1)
-            build(bounds[-1], g_steps)
         flux = product(it)
     flux_out[...] = flux
 

time: 105 us -> 101 us (0.962)
  Pallas kernels: 104 us -> 100 us
    pallas_call x1, Pallas kernels: 102 us -> 98.2 us  [per_device(): pl.pallas_call(functools.partial(kernel, plan), out_shape=(jax.ShapeDtype...]
where the time goes in v3:
time: 101 us
  Pallas kernels  100 us (99%)
    pallas_call x1, Pallas kernels, per_device(): pl.pallas_call(functools.partial(kernel, plan), out_shape=(jax.ShapeDtype...  98.2 us

profile of v3, /device:TPU:1, one launch (start us, length us, event | category | flops | bytes accessed | tf_op | source)
XLA Modules:
  0.0 100.9 jit_solution(15187869486600062922)
XLA Ops:
  0.6 98.2 %coupled.1 = (f32[8,8,16,128]{3,2,1,0:T(8,128)}, f32[16,128]{1,0:T(8,128)}) custom-call(f32[16,8,8,128]{3,2,1,0:T(8,128)} %source.1, s32[8,8,128]{2,1,0:T(8,128)} %labels.1, f32[8]{0:T(128)} %coeff.1, s32[1,128]{1,0:T(1,128)} %bitcast.1, f32[3,128]{1,0:T(4,128)} %pos.1, f32[16,128]{1,0:T(8,128)} %incident.1), custom_call_target="tpu_custom_call" | custom-call | tf_op jit(solution)/shard_map/coupled/pallas_call | solution.py:503
  98.9 1.9 %write_out.1 = (f32[16,8,8,128]{3,2,1,0:T(8,128)}, f32[16,128]{1,0:T(8,128)}) custom-call(f32[8,8,16,128]{3,2,1,0:T(8,128)} %get-tuple-element.4.field, f32[16,128]{1,0:T(8,128)} %get-tuple-element.5.flux), custom_call_target="tpu_custom_call" | custom-call | tf_op jit(solution)/shard_map/write_out/pallas_call | solution.py:551
